TPU v7x, 32 devices: a whole 2x2x4 slice. The times are simulated.
32 devices in a mesh: pair: 8 (over z, y), band: 4 (over x, core).
Axes of the slice: x: 2, y: 2, z: 4, core: 2. Of those that a mesh axis runs over, the one named last changes fastest.
Arguments:
- orbitals: bfloat16 [2048, 23, 64], P('pair'), may hold values from -6 to 6
- screening: bfloat16 [1024, 8, 1024], P('pair', None, 'band'), may hold values from -0.1875 to 0.1875
- trial: bfloat16 [1024, 23, 64], P('pair'), may hold values from -6 to 6
- pair_kpts: int32 [8, 2], replicated, may hold values from 0 to 22
- pair_q: int32 [8], replicated, may hold values from 0 to 7
Outputs:
- applied: float32 [1024, 23, 64], P('pair', None, 'band')
All inputs are finite; a program needn't handle non-finite values.
Results may differ from a plain program's by a relative error of at most 0.013.
Values may be sent and summed in bfloat16 or wider, within the bound.
No kernel may reach another device: no remote copies, remote signals or barrier semaphores. Data moves between devices by JAX's collectives and lax.ppermute only.
A program may use at most 64 MiB of HBM per device.

v0:
```python
import math

import jax
import jax.numpy as jnp
from jax import lax
from jax.experimental import pallas as pl
from jax.experimental.pallas import tpu as pltpu
from jax.sharding import Mesh, PartitionSpec as P


NV = 32
NC = 32
NR = 2048
NG = 1024
NVC = NV * NC
LANES = 128
HALVES = 2
TABLE = 32
F32 = jnp.float32
BF16 = jnp.bfloat16
VMEM_LIMIT = 40 * 1024 * 1024


def dot(a, b):
    return lax.dot_general(a, b, (((1,), (0,)), ((), ())), preferred_element_type=F32)


def dot_rows(a, b):
    return lax.dot_general(a, b, (((1,), (1,)), ((), ())), preferred_element_type=F32)


SPACES = {"s": pltpu.SMEM, "v": pltpu.VMEM, "h": pl.ANY}


def call(body, inputs, outputs, scratch=(), flops=0):
    specs, arrays = [], []
    for space, array in inputs:
        specs.append(pl.BlockSpec(memory_space=SPACES.get(space, pltpu.VMEM)))
        home = pltpu.VMEM if space == "v" else pltpu.HBM
        array = pltpu.with_memory_space_constraint(array, home)
        arrays.append(array)
    shapes, out_specs = [], []
    for space, shape, dtype in outputs:
        kind = {"v": pltpu.VMEM, "h": pltpu.HBM}.get(space, jax.ShapeDtypeStruct)
        shapes.append(kind(shape, dtype))
        out_specs.append(pl.BlockSpec(memory_space=SPACES.get(space, pltpu.VMEM)))
    return pl.pallas_call(
        body,
        out_shape=shapes,
        in_specs=specs,
        out_specs=out_specs,
        scratch_shapes=list(scratch),
        compiler_params=pltpu.CompilerParams(vmem_limit_bytes=VMEM_LIMIT),
        cost_estimate=pl.CostEstimate(flops=int(flops), transcendentals=0, bytes_accessed=1 << 20),
    )(*arrays)


def pack_kernel(kpts_ref, orbital_ref, trial_ref, out_ref, room, fetch_sems, send_sems):
    bx, bc = lax.axis_index("bx"), lax.axis_index("bc")
    strips, low = lax.axis_size("bx"), room.shape[0]
    points = orbital_ref.shape[2]
    bands = pl.ds(pl.multiple_of(bc * NV, NV), NV)
    fetches = []
    for d in range(low):
        pair = d * strips + bx
        first, second, own = kpts_ref[0, pair], kpts_ref[1, pair], kpts_ref[bc, pair]
        parts = (
            (orbital_ref.at[first, bands, :], room.at[d, pl.ds(0, NV), pl.ds(0, points)]),
            (orbital_ref.at[second, bands, :], room.at[d, pl.ds(NV, NV), pl.ds(0, points)]),
            (trial_ref.at[own], room.at[d, :, pl.ds(points, trial_ref.shape[2])]),
        )
        fetches.append([pltpu.make_async_copy(x, y, fetch_sems.at[d, k]) for k, (x, y) in enumerate(parts)])
        for fetch in fetches[-1]:
            fetch.start()
    sends = []
    for d in range(low):
        for fetch in fetches[d]:
            fetch.wait()
        for h in range(out_ref.shape[0] // low):
            sends.append(pltpu.make_async_copy(room.at[d], out_ref.at[h * low + d], send_sems.at[h, d]))
            sends[-1].start()
    for send in sends:
        send.wait()


def basis_kernel(out_ref, cos_low, sin_low, cos_high, sin_high, rows, sems):
    columns = rows.shape[1]
    quarter = columns // 4
    groups = lax.axis_size("bc")
    strip = NG // (lax.axis_size("bx") * groups)
    column = lax.broadcasted_iota(jnp.int32, (1, columns), 1)
    odd = column // quarter % 2
    inner = column % quarter
    frequency = jnp.where(
        column < 2 * quarter,
        lax.axis_index("ph") * 2 * quarter + 2 * inner,
        (inner // (strip // 2) * groups + lax.axis_index("bc")) * strip + 2 * (inner % (strip // 2)),
    ) + odd
    period = 4 * NR
    unit = math.pi / (2 * NR)
    fine = 8

    def turn(count, step, offset):
        multiple = lax.broadcasted_iota(jnp.int32, (count, columns), 0) * step + offset
        index = multiple * frequency & (period - 1)
        angle = jnp.where(index >= period // 2, index - period, index).astype(F32) * unit
        return jnp.cos(angle), jnp.sin(angle)

    def table(step, offset, cos_ref, sin_ref, scale):
        cos_a, sin_a = turn(fine, step, offset)
        cos_b, sin_b = turn(TABLE // fine, step * fine, 0)
        cos_a, sin_a = cos_a * scale, sin_a * scale
        for k in range(TABLE // fine):
            c, s = cos_b[k : k + 1], sin_b[k : k + 1]
            cos_ref[k * fine : (k + 1) * fine, :] = cos_a * c - sin_a * s
            sin_ref[k * fine : (k + 1) * fine, :] = sin_a * c + cos_a * s

    table(2, 1, cos_low, sin_low, math.sqrt(2.0 / NR))
    table(2 * TABLE, 0, cos_high, sin_high, 1.0)
    parts = sems.shape[0]
    blocks = rows.shape[0] // TABLE // parts
    copies = []
    for part in range(parts):

        def step(block, carry):
            high = pl.ds(block, 1)
            value = cos_low[...] * cos_high[high, :] - sin_low[...] * sin_high[high, :]
            rows[pl.ds(pl.multiple_of(block * TABLE, TABLE), TABLE), :] = value.astype(BF16)
            return carry

        lax.fori_loop(part * blocks, (part + 1) * blocks, step, 0)
        span = pl.ds(part * blocks * TABLE, blocks * TABLE)
        copies.append(pltpu.make_async_copy(rows.at[span, :], out_ref.at[span, :], sems.at[part]))
        copies[-1].start()
    for copy in copies:
        copy.wait()


def select_kernel(q_ref, screen_ref, *refs):
    sends, ordered = refs[:-1], refs[-1]
    me = lax.axis_index(("pl", "bx"))
    rows, columns = sends[0].shape
    kinds = screen_ref.shape[0] // rows
    source = lax.broadcasted_iota(jnp.int32, (columns, columns), 0)
    target = lax.broadcasted_iota(jnp.int32, (columns, columns), 1)
    wanted = target % (columns // 2) * 2 + target // (columns // 2)
    order = jnp.where(source == wanted, 1.0, 0.0).astype(BF16)
    result = dot(screen_ref[...], order)
    for t in range(columns // LANES):
        ordered[t] = result[:, t * LANES : (t + 1) * LANES]
    for distance, send in enumerate(sends):
        q = q_ref[me ^ distance]
        for odd in range(2):
            for t in range(columns // LANES):
                send[odd * rows // 2 : (odd + 1) * rows // 2, t * LANES : (t + 1) * LANES] = ordered[
                    t, pl.ds(q + kinds * odd, rows // 2, stride=2 * kinds), :
                ].astype(BF16)


def transform_kernel(
    own_ref,
    other_ref,
    basis_ref,
    val_ref,
    cond_ref,
    first,
    second,
    even,
    odd,
    basis,
    conduction,
    sems,
):
    side = lax.axis_index("bc")
    blocks, _, _ = own_ref.shape
    points = NR // blocks
    piece = 256 if points % 256 == 0 else LANES
    middle = NR // 2
    half = val_ref.shape[1]
    quarter = half // 2
    strips = lax.axis_size("bx")
    run = quarter // strips
    fetches = [
        pltpu.make_async_copy(basis_ref.at[:, pl.ds(k * half, half)], basis.at[k], sems.at[k]) for k in range(2)
    ]
    fetches[1].start()
    fetches[0].start()
    source = lax.broadcasted_iota(jnp.int32, (piece, piece), 0)
    target = lax.broadcasted_iota(jnp.int32, (piece, piece), 1)
    flip = jnp.where(source + target == piece - 1, 1.0, 0.0).astype(BF16)
    for slot, ref in ((side, own_ref), (1 - side, other_ref)):
        for start in range(0, middle, piece):
            ahead = ref[start // points, :, start % points : start % points + piece].astype(F32)
            mirror = NR - start - piece
            behind = dot(ref[mirror // points, :, mirror % points : mirror % points + piece], flip)
            for half_of, value in enumerate((ahead, behind)):
                first[slot, half_of, :, start : start + piece] = value[:NV]
                second[slot, half_of, :, start : start + piece] = value[NV:]

    store = pltpu.make_async_copy(conduction, cond_ref, sems.at[2])
    for kind in (1, 0):
        outer, inner = (second, first) if kind else (first, second)
        for v in range(NV):
            rows = slice(v * NV, (v + 1) * NV)
            ahead = outer[kind, 0, v : v + 1, :] * inner[kind, 0]
            behind = outer[kind, 1, v : v + 1, :] * inner[kind, 1]
            even[kind, rows, :] = (ahead + behind).astype(BF16)
            odd[kind, rows, :] = (ahead - behind).astype(BF16)
        fetches[kind].wait()
        for parity, density in enumerate((even, odd)):
            result = dot(density[kind], basis[kind, :, parity * quarter : (parity + 1) * quarter]).astype(BF16)
            if kind == 0:
                val_ref[:, parity * quarter : (parity + 1) * quarter] = result
            else:
                for s in range(strips):
                    to = (2 * s + parity) * run
                    conduction[:, to : to + run] = result[:, s * run : (s + 1) * run]
        if kind == 1:
            store.start()
    store.wait()


def apply_kernel(own_ref, other_ref, val_ref, cond_ref, *refs):
    *screens, out_ref, screen, screened, slabs, vectors, diagonal, conduction, sides, sem = refs
    fetch = pltpu.make_async_copy(cond_ref, conduction, sem)
    fetch.start()
    side = lax.axis_index("bc")
    blocks, count, width = own_ref.shape
    states = NVC // blocks
    half = val_ref.shape[1]
    strips = lax.axis_size("bx")
    broad = screen.shape[2]
    if len(screens) > 1:
        me = lax.axis_index(("pl", "bx"))
        part = screens[0].shape[0] // 2
        for distance, ref in enumerate(screens):
            origin = me ^ distance
            for odd in range(2):
                at = pl.multiple_of(odd * (half // 2) + origin // strips * part, part)
                screen[origin % strips, pl.ds(at, part), :] = ref[odd * part : (odd + 1) * part, :]
    else:
        screen[...] = screens[0][...]
    for s in range(strips):
        screened[:, s * broad : (s + 1) * broad] = dot(val_ref[...], screen[s]).astype(BF16)

    repeat = LANES // NV
    lanes = repeat * count
    fold = LANES // count
    lane = lax.broadcasted_iota(jnp.int32, (NV, lanes), 1) // count
    masks = [jnp.where(lane == r, 1.0, 0.0).astype(BF16) for r in range(repeat)]
    for b in range(blocks):
        for slot, ref in ((side, own_ref), (1 - side, other_ref)):
            turned = ref[b, :, width - states :].astype(F32).T
            vectors[slot, b * states : (b + 1) * states, :] = jnp.concatenate([turned] * fold, axis=1)
    groups = NVC // LANES
    scale = 1.0 / math.sqrt(NVC) / math.sqrt(NG)
    source = lax.broadcasted_iota(jnp.int32, (LANES, LANES), 0)
    target = lax.broadcasted_iota(jnp.int32, (LANES, LANES), 1)
    weave = jnp.where(target == source % NV * repeat + source // NV, 1.0, 0.0).astype(BF16)

    def put(kind, i, value):
        if len(out_ref.shape) == 3:
            out_ref[kind, :, i * LANES : (i + 1) * LANES] = value
        else:
            share, states = out_ref.shape[3:]
            to, at = i * LANES // states, i * LANES % states
            for b in range(out_ref.shape[1]):
                out_ref[to, b, kind, :, at : at + LANES] = value[b * share : (b + 1) * share]

    fetch.wait()
    for kind in range(2):
        for j in range(NC):
            rows = vectors[1, pl.ds(j, NV, stride=NV), :] if kind == 0 else vectors[0, j * NC : (j + 1) * NC, :]
            rows = jnp.concatenate([rows.astype(BF16)] * (lanes // LANES), axis=1)
            for r in range(repeat):
                diagonal[kind, j * LANES + r * NV : j * LANES + (r + 1) * NV, :] = rows * masks[r]
        left, right = (conduction, screened) if kind == 0 else (screened, conduction)
        raw = dot_rows(left[...], right[...]).astype(BF16)
        for j in range(NC):
            for g in range(groups):
                slabs[kind, g * NC : (g + 1) * NC, j * LANES : (j + 1) * LANES] = raw[
                    j * NC : (j + 1) * NC, g * LANES : (g + 1) * LANES
                ]
        total = dot(slabs[kind], diagonal[kind]) * scale
        if kind == 0:
            for g in range(groups):
                block = total[g * NC : (g + 1) * NC, :]
                stacked = jnp.concatenate([block[:, r * count : (r + 1) * count] for r in range(repeat)], axis=0)
                put(0, g, stacked.T.astype(BF16))
            continue
        for t in range(lanes // LANES):
            sides[t] = total[:, t * LANES : (t + 1) * LANES]
        for at in range(0, groups, fold):
            strands = []
            for r in range(repeat):
                for w in range(repeat):
                    pieces = [
                        sides[r // fold, pl.ds((at + f) * repeat + w, groups, stride=NV), :][
                            :, r % fold * count : (r % fold + 1) * count
                        ]
                        for f in range(fold)
                    ]
                    strands.append(jnp.concatenate(pieces, axis=1))
            stacked = jnp.concatenate(strands, axis=0).astype(BF16)
            woven = lax.dot_general(stacked, weave, (((0,), (0,)), ((), ())), preferred_element_type=F32)
            for f in range(fold):
                put(1, at + f, woven[f * count : (f + 1) * count].astype(BF16))


def gather_kernel(kpts_ref, got_ref, out_ref):
    out_ref[...] = jnp.zeros_like(out_ref)
    halves, low, strips, groups = got_ref.shape[:4]
    for p in range(low * strips):
        for s in range(2):
            total = None
            for h in range(halves):
                for g in range(groups):
                    part = got_ref[h, p // strips, p % strips, g, s].astype(F32)
                    total = part if total is None else total + part
            k = kpts_ref[s, p]
            out_ref[k] += total


def on_device(orbitals, screening, trial, pair_kpts, pair_q):
    halves, low, strips, groups = (lax.axis_size(a) for a in ("ph", "pl", "bx", "bc"))
    pair_axes, all_axes = ("ph", "pl"), ("ph", "pl", "bx", "bc")
    pair_count = halves * low
    points, kpt_count, _ = orbitals.shape
    states, _, count = trial.shape
    tall, kinds, broad = screening.shape
    half = NG // HALVES
    aligned = points % LANES == 0 and states % LANES == 0
    orbital_t, trial_t = orbitals.transpose(1, 2, 0), trial.transpose(1, 2, 0)
    kpts_t = pair_kpts.T

    if aligned:
        send = call(
            pack_kernel,
            [("s", kpts_t), ("h", orbital_t), ("h", trial_t)],
            [("h", (pair_count, count, points + states), BF16)],
            [
                pltpu.VMEM((low, count, points + states), BF16),
                pltpu.SemaphoreType.DMA((low, 3)),
                pltpu.SemaphoreType.DMA((halves, low)),
            ],
        )[0]
        screen_sends = call(
            select_kernel,
            [("s", pair_q), ("b", screening.reshape(tall * kinds, broad))],
            [("b", (tall, broad), BF16)] * (low * strips),
            [pltpu.VMEM((broad // LANES, tall * kinds, LANES), F32)],
            flops=NG * NG * 256,
        )
    else:
        bx, bc = lax.axis_index("bx"), lax.axis_index("bc")
        near = lax.dynamic_index_in_dim(pair_kpts.reshape(low, strips, 2), bx, 1, keepdims=False)
        orbital_half = lax.dynamic_slice_in_dim(orbital_t, bc * NV, NV, 1)
        orbital_part = orbital_half[near].reshape(low, 2 * NV, points)
        trial_part = trial_t[lax.dynamic_index_in_dim(near, bc, 1, keepdims=False)]
        send = jnp.concatenate([orbital_part, trial_part], axis=2)
        send = jnp.concatenate([send] * halves, axis=0)
        screen_send = screening.transpose(1, 0, 2)[pair_q]
    got = lax.all_to_all(send, pair_axes, split_axis=0, concat_axis=0, tiled=True)
    basis = call(
        basis_kernel,
        [],
        [("h", (NR // 2, 2 * half), BF16)],
        [pltpu.VMEM((TABLE, 2 * half), F32)] * 4
        + [pltpu.VMEM((NR // 2, 2 * half), BF16), pltpu.SemaphoreType.DMA((4,))],
        flops=NR * NG * 8,
    )[0]
    if aligned:
        near_axes = ("pl", "bx")
        screens = list(screen_sends[:1])
        for distance in range(1, low * strips):
            to = [(i, i ^ distance) for i in range(low * strips)]
            screens.append(lax.ppermute(screen_sends[distance], near_axes, to))
    else:
        screen_got = lax.all_to_all(screen_send, ("pl", "bx"), split_axis=0, concat_axis=0, tiled=True)
    other = lax.ppermute(got, "bc", [(i, i ^ 1) for i in range(groups)])

    if not aligned:

        def joined(x):
            turned = x.transpose(1, 0, 2)
            return jnp.concatenate(
                [turned[:, :, :points].reshape(1, count, NR), turned[:, :, points:].reshape(1, count, NVC)], axis=2
            )

        got, other = joined(got), joined(other)
        screen_got = screen_got.reshape(low, strips, tall // 2, 2, broad // 2, 2).transpose(1, 3, 0, 2, 5, 4)
        screens = [screen_got.reshape(strips, low * tall, broad)]

    valence, conduction = call(
        transform_kernel,
        [("v", got), ("v", other), ("h", basis)],
        [("v", (NVC, half), BF16), ("h", (NVC, half), BF16)],
        [
            pltpu.VMEM((2, 2, NV, NR // 2), F32),
            pltpu.VMEM((2, 2, NV, NR // 2), F32),
            pltpu.VMEM((2, NVC, NR // 2), BF16),
            pltpu.VMEM((2, NVC, NR // 2), BF16),
            pltpu.VMEM((2, NR // 2, half), BF16),
            pltpu.VMEM((NVC, half), BF16),
            pltpu.SemaphoreType.DMA((3,)),
        ],
        flops=2 * NVC * NR * half,
    )
    share = count // (strips * groups)
    lanes = LANES // NV * count
    partial = call(
        apply_kernel,
        [("v", got), ("v", other), ("v", valence), ("h", conduction)] + [("v", x) for x in screens],
        [("v", (pair_count, strips * groups, 2, share, states) if aligned else (2, count, NVC), BF16)],
        [
            pltpu.VMEM((strips, half, broad), BF16),
            pltpu.VMEM((NVC, half), BF16),
            pltpu.VMEM((2, NVC // LANES * NC, NC * LANES), BF16),
            pltpu.VMEM((2, NVC, LANES), F32),
            pltpu.VMEM((2, NC * LANES, lanes), BF16),
            pltpu.VMEM((NVC, half), BF16),
            pltpu.VMEM((lanes // LANES, NVC // LANES * NC, LANES), F32),
            pltpu.SemaphoreType.DMA,
        ],
        flops=2 * NVC * half * half + 8 * NVC * NVC * half,
    )[0]
    if not aligned:
        partial = partial.reshape(2, strips * groups, share, pair_count, states).transpose(3, 1, 0, 2, 4)
    out_send = partial.reshape(pair_count * strips * groups, 2, share, states)
    out_got = lax.all_to_all(out_send, all_axes, split_axis=0, concat_axis=0, tiled=True)
    out_got = out_got.reshape(halves, low, strips, groups, 2, share, states)
    if aligned:
        applied = call(gather_kernel, [("s", kpts_t), ("v", out_got)], [("b", (kpt_count, share, states), F32)])[0]
    else:
        summed = jnp.sum(out_got.astype(F32), axis=(0, 3)).reshape(-1, share * states)
        hot = (pair_kpts.reshape(-1)[None, :] == jnp.arange(kpt_count)[:, None]).astype(F32)
        applied = lax.dot_general(
            hot, summed, (((1,), (0,)), ((), ())), precision=lax.Precision.HIGHEST, preferred_element_type=F32
        ).reshape(kpt_count, share, states)
    return applied.transpose(2, 0, 1)


def solution(mesh):
    pair_count, band_count = mesh.shape["pair"], mesh.shape["band"]
    shape = (HALVES, pair_count // HALVES, 2, band_count // 2)
    fine = Mesh(mesh.devices.reshape(shape), ("ph", "pl", "bx", "bc"))
    pair_axes, band_axes = ("ph", "pl"), ("bx", "bc")
    return jax.shard_map(
        on_device,
        mesh=fine,
        in_specs=(
            P(pair_axes, None, None),
            P(pair_axes, None, band_axes),
            P(pair_axes, None, None),
            P(),
            P(),
        ),
        out_specs=P(pair_axes, None, band_axes),
        check_vma=False,
    )
```

profile of v0, /device:TPU:0, one launch (start us, length us, event | category | flops | bytes accessed | tf_op | source)
XLA Modules:
  0.0 62.8 jit_solution(11099211433563929747)
XLA Ops:
  0.0 2.4 %shard_map.55 = bf16[8,64,384]{2,1,0:T(8,128)(2,1)} custom-call(s32[2,8]{1,0:T(2,128)} %bitcast.11, bf16[23,64,256]{2,1,0:T(8,128)(2,1)} %bitcast.9, bf16[23,64,128]{2,1,0:T(8,128)(2,1)} %bitcast.10), custom_call_target="tpu_custom_call" | custom-call | bytes 1048576 | tf_op jit(solution)/shard_map/pallas_call | solution.py:47
  2.4 19.4 %all_to_all.10.own_ref = bf16[8,64,384]{2,1,0:T(8,128)(2,1)S(1)} all-to-all(bf16[8,64,384]{2,1,0:T(8,128)(2,1)} %shard_map.55), channel_id=1, replica_groups=mesh['ph'=2,'pl'=4,'bx'=2,'bc'=2] {'ph','pl'}, dimensions={0} | all-to-all | bytes 786432 | tf_op jit(solution)/shard_map/all_to_all | solution.py:363
  21.8 0.0 collective-permute-start
  21.8 1.7 %shard_map.58 = (bf16[128,256]{1,0:T(8,128)(2,1)S(1)}, bf16[128,256]{1,0:T(8,128)(2,1)S(1)}, bf16[128,256]{1,0:T(8,128)(2,1)S(1)}, bf16[128,256]{1,0:T(8,128)(2,...) custom-call(s32[8]{0:T(128)} %q_ref.1, ...), custom_call_target="tpu_custom_call" | custom-call | flops 268435456 | bytes 1048576 | tf_op jit(solution)/shard_map/pallas_call | solution.py:47
  23.5 1.6 %collective-permute-start.1 = (bf16[128,256]{1,0:T(8,128)(2,1)S(1)}, bf16[128,256]{1,0:T(8,128)(2,1)S(1)}, u32[]{:S(2)}, u32[]{:S(2)}) collective-permute-start(bf16[128,256]{1,0:T(8,128)(2,1)S(1)} %get-tuple-element.18), channel_id=1, source_target_pairs={{0,2},{2,0},{4,6},{6,4},{8,10},{10,8},{12,14},{14,12},{1,3},{3,1},... | collective-permute-start | bytes 196616 | tf_op jit(solution)/shard_map/ppermute | solution.py:377
  25.1 1.1 %collective-permute-start.2 = (bf16[128,256]{1,0:T(8,128)(2,1)S(1)}, bf16[128,256]{1,0:T(8,128)(2,1)S(1)}, u32[]{:S(2)}, u32[]{:S(2)}) collective-permute-start(bf16[128,256]{1,0:T(8,128)(2,1)S(1)} %get-tuple-element.19), channel_id=1, source_target_pairs={{0,4},{2,6},{4,0},{6,2},{8,12},{10,14},{12,8},{14,10},{1,5},{3,7},... | collective-permute-start | bytes 196616 | tf_op jit(solution)/shard_map/ppermute | solution.py:377
  26.1 0.9 %collective-permute-start.3 = (bf16[128,256]{1,0:T(8,128)(2,1)S(1)}, bf16[128,256]{1,0:T(8,128)(2,1)S(1)}, u32[]{:S(2)}, u32[]{:S(2)}) collective-permute-start(bf16[128,256]{1,0:T(8,128)(2,1)S(1)} %get-tuple-element.20), channel_id=1, source_target_pairs={{0,6},{2,4},{4,2},{6,0},{8,14},{10,12},{12,10},{14,8},{1,7},{3,5},... | collective-permute-start | bytes 196616 | tf_op jit(solution)/shard_map/ppermute | solution.py:377
  27.1 0.9 %collective-permute-start.4 = (bf16[128,256]{1,0:T(8,128)(2,1)S(1)}, bf16[128,256]{1,0:T(8,128)(2,1)S(1)}, u32[]{:S(2)}, u32[]{:S(2)}) collective-permute-start(bf16[128,256]{1,0:T(8,128)(2,1)S(1)} %get-tuple-element.21), channel_id=1, source_target_pairs={{0,8},{2,10},{4,12},{6,14},{8,0},{10,2},{12,4},{14,6},{1,9},{3,11}... | collective-permute-start | bytes 196616 | tf_op jit(solution)/shard_map/ppermute | solution.py:377
  28.0 2.2 %shard_map.56.basis_ref = bf16[1024,1024]{1,0:T(8,128)(2,1)} custom-call(), custom_call_target="tpu_custom_call" | custom-call | flops 16777216 | bytes 1048576 | tf_op jit(solution)/shard_map/pallas_call | solution.py:47
  30.2 0.0 collective-permute-done.1.refs_1_
  30.2 2.1 %collective-permute-start.5 = (bf16[128,256]{1,0:T(8,128)(2,1)S(1)}, bf16[128,256]{1,0:T(8,128)(2,1)S(1)}, u32[]{:S(2)}, u32[]{:S(2)}) collective-permute-start(bf16[128,256]{1,0:T(8,128)(2,1)S(1)} %get-tuple-element.22), channel_id=1, source_target_pairs={{0,10},{2,8},{4,14},{6,12},{8,2},{10,0},{12,6},{14,4},{1,11},{3,9}... | collective-permute-start | bytes 196616 | tf_op jit(solution)/shard_map/ppermute | solution.py:377
  32.3 0.0 collective-permute-done.2.refs_2_
  32.3 0.7 %collective-permute-start.6 = (bf16[128,256]{1,0:T(8,128)(2,1)S(1)}, bf16[128,256]{1,0:T(8,128)(2,1)S(1)}, u32[]{:S(2)}, u32[]{:S(2)}) collective-permute-start(bf16[128,256]{1,0:T(8,128)(2,1)S(1)} %get-tuple-element.23), channel_id=1, source_target_pairs={{0,12},{2,14},{4,8},{6,10},{8,4},{10,6},{12,0},{14,2},{1,13},{3,15... | collective-permute-start | bytes 196616 | tf_op jit(solution)/shard_map/ppermute | solution.py:377
  33.1 0.0 collective-permute-done.other_ref
  33.1 2.2 %collective-permute-start.7 = (bf16[128,256]{1,0:T(8,128)(2,1)S(1)}, bf16[128,256]{1,0:T(8,128)(2,1)S(1)}, u32[]{:S(2)}, u32[]{:S(2)}) collective-permute-start(bf16[128,256]{1,0:T(8,128)(2,1)S(1)} %get-tuple-element.24), channel_id=1, source_target_pairs={{0,14},{2,12},{4,10},{6,8},{8,6},{10,4},{12,2},{14,0},{1,15},{3,13... | collective-permute-start | bytes 196616 | tf_op jit(solution)/shard_map/ppermute | solution.py:377
  35.2 5.7 %shard_map.57 = (bf16[1024,512]{1,0:T(8,128)(2,1)S(1)}, bf16[1024,512]{1,0:T(8,128)(2,1)}) custom-call(bf16[8,64,384]{2,1,0:T(8,128)(2,1)S(1)} %all_to_all.10.own_ref, bf16[8,64,384]{2,1,0:T(8,128)(2,1)S(1)} %collective-permute-done.other_ref, bf16[1024,1024]{1,0:T(8,128)(2,1)} %shard_map.56.basis_ref), custom_call_target="tpu_custom_call" | custom-call | flops 2147483648 | bytes 1048576 | tf_op jit(solution)/shard_map/pallas_call | solution.py:47
  40.9 0.0 collective-permute-done.3.refs_3_
  40.9 0.0 collective-permute-done.4.refs_4_
  40.9 0.0 collective-permute-done.5.refs_5_
  40.9 0.0 collective-permute-done.6.refs_6_
  41.0 0.0 collective-permute-done.7.refs_7_
  41.0 6.7 %shard_map.59 = bf16[8,4,2,16,128]{4,3,2,1,0:T(8,128)(2,1)S(1)} custom-call(bf16[8,64,384]{2,1,0:T(8,128)(2,1)S(1)} %all_to_all.10.own_ref, bf16[8,64,384]{2,1,0:T(8,128)(2,1)S(1)} %collective-permute-done.other_ref, bf16[1024,512]{1,0:T(8,128)(2,1)S(1)} %get-tuple-element.15.val_ref, bf16[1024,512]{1,0:T(8,128)(2,1)} %get-tuple-element.16.cond_ref, ...), custom_call_target="tpu_custom_call" | custom-call | flops 4831838208 | bytes 1048576 | tf_op jit(solution)/shard_map/pallas_call | solution.py:47
  47.7 13.7 %all_to_all.11 = bf16[32,2,16,128]{3,2,1,0:T(8,128)(2,1)S(1)} all-to-all(bf16[32,2,16,128]{3,2,1,0:T(8,128)(2,1)S(1)} %bitcast.8), channel_id=1, replica_groups=mesh['ph'=2,'pl'=4,'bx'=2,'bc'=2] {'ph','pl','bx','bc'}, dimensions={0} | all-to-all | bytes 524288 | tf_op jit(solution)/shard_map/all_to_all | solution.py:430
  61.3 1.4 %shard_map.60 = f32[23,16,128]{2,1,0:T(8,128)} custom-call(s32[2,8]{1,0:T(2,128)} %bitcast.12, bf16[2,4,2,2,2,16,128]{6,5,4,3,2,1,0:T(8,128)(2,1)S(1)} %bitcast.7), custom_call_target="tpu_custom_call" | custom-call | bytes 1048576 | tf_op jit(solution)/shard_map/pallas_call | solution.py:47
Async XLA Ops:
  21.8 11.3 %collective-permute-start = (bf16[8,64,384]{2,1,0:T(8,128)(2,1)S(1)}, bf16[8,64,384]{2,1,0:T(8,128)(2,1)S(1)}, u32[]{:S(2)}, u32[]{:S(2)}) collective-permute-start(bf16[8,64,384]{2,1,0:T(8,128)(2,1)S(1)} %all_to_all.10.own_ref), channel_id=1, source_target_pairs={{0,1},{1,0},{2,3},{3,2},{4,5},{5,4},{6,7},{7,6},{8,9},{9,8},{10,11... | collective-permute-start | bytes 1179656 | tf_op jit(solution)/shard_map/ppermute | solution.py:380
  23.5 6.7 %collective-permute-start.1 = (bf16[128,256]{1,0:T(8,128)(2,1)S(1)}, bf16[128,256]{1,0:T(8,128)(2,1)S(1)}, u32[]{:S(2)}, u32[]{:S(2)}) collective-permute-start(bf16[128,256]{1,0:T(8,128)(2,1)S(1)} %get-tuple-element.18), channel_id=1, source_target_pairs={{0,2},{2,0},{4,6},{6,4},{8,10},{10,8},{12,14},{14,12},{1,3},{3,1},... | collective-permute-start | bytes 196616 | tf_op jit(solution)/shard_map/ppermute | solution.py:377
  25.1 7.3 %collective-permute-start.2 = (bf16[128,256]{1,0:T(8,128)(2,1)S(1)}, bf16[128,256]{1,0:T(8,128)(2,1)S(1)}, u32[]{:S(2)}, u32[]{:S(2)}) collective-permute-start(bf16[128,256]{1,0:T(8,128)(2,1)S(1)} %get-tuple-element.19), channel_id=1, source_target_pairs={{0,4},{2,6},{4,0},{6,2},{8,12},{10,14},{12,8},{14,10},{1,5},{3,7},... | collective-permute-start | bytes 196616 | tf_op jit(solution)/shard_map/ppermute | solution.py:377
  26.1 14.8 %collective-permute-start.3 = (bf16[128,256]{1,0:T(8,128)(2,1)S(1)}, bf16[128,256]{1,0:T(8,128)(2,1)S(1)}, u32[]{:S(2)}, u32[]{:S(2)}) collective-permute-start(bf16[128,256]{1,0:T(8,128)(2,1)S(1)} %get-tuple-element.20), channel_id=1, source_target_pairs={{0,6},{2,4},{4,2},{6,0},{8,14},{10,12},{12,10},{14,8},{1,7},{3,5},... | collective-permute-start | bytes 196616 | tf_op jit(solution)/shard_map/ppermute | solution.py:377
  27.1 13.9 %collective-permute-start.4 = (bf16[128,256]{1,0:T(8,128)(2,1)S(1)}, bf16[128,256]{1,0:T(8,128)(2,1)S(1)}, u32[]{:S(2)}, u32[]{:S(2)}) collective-permute-start(bf16[128,256]{1,0:T(8,128)(2,1)S(1)} %get-tuple-element.21), channel_id=1, source_target_pairs={{0,8},{2,10},{4,12},{6,14},{8,0},{10,2},{12,4},{14,6},{1,9},{3,11}... | collective-permute-start | bytes 196616 | tf_op jit(solution)/shard_map/ppermute | solution.py:377
  30.2 10.7 %collective-permute-start.5 = (bf16[128,256]{1,0:T(8,128)(2,1)S(1)}, bf16[128,256]{1,0:T(8,128)(2,1)S(1)}, u32[]{:S(2)}, u32[]{:S(2)}) collective-permute-start(bf16[128,256]{1,0:T(8,128)(2,1)S(1)} %get-tuple-element.22), channel_id=1, source_target_pairs={{0,10},{2,8},{4,14},{6,12},{8,2},{10,0},{12,6},{14,4},{1,11},{3,9}... | collective-permute-start | bytes 196616 | tf_op jit(solution)/shard_map/ppermute | solution.py:377
  32.3 8.6 %collective-permute-start.6 = (bf16[128,256]{1,0:T(8,128)(2,1)S(1)}, bf16[128,256]{1,0:T(8,128)(2,1)S(1)}, u32[]{:S(2)}, u32[]{:S(2)}) collective-permute-start(bf16[128,256]{1,0:T(8,128)(2,1)S(1)} %get-tuple-element.23), channel_id=1, source_target_pairs={{0,12},{2,14},{4,8},{6,10},{8,4},{10,6},{12,0},{14,2},{1,13},{3,15... | collective-permute-start | bytes 196616 | tf_op jit(solution)/shard_map/ppermute | solution.py:377
  33.1 7.9 %collective-permute-start.7 = (bf16[128,256]{1,0:T(8,128)(2,1)S(1)}, bf16[128,256]{1,0:T(8,128)(2,1)S(1)}, u32[]{:S(2)}, u32[]{:S(2)}) collective-permute-start(bf16[128,256]{1,0:T(8,128)(2,1)S(1)} %get-tuple-element.24), channel_id=1, source_target_pairs={{0,14},{2,12},{4,10},{6,8},{8,6},{10,4},{12,2},{14,0},{1,15},{3,13... | collective-permute-start | bytes 196616 | tf_op jit(solution)/shard_map/ppermute | solution.py:377
where the time goes:
time: 63.2 us; the launch traced here: 62.8 us
  blocking collectives  33 us (52%)
  Pallas kernels  20.1 us (32%)
  starting transfers between devices  9.47 us (15%)
    pallas_call x6, Pallas kernels, call(): pl.pallas_call(body, out_shape=shapes, in_specs=specs, out_specs=out_spec...  20.1 us
    all_to_all x1, blocking collectives, on_device(): lax.all_to_all(send, pair_axes, split_axis=0, concat_axis=0, tiled=True)  19.4 us
    all_to_all x1, blocking collectives, on_device(): lax.all_to_all(out_send, all_axes, split_axis=0, concat_axis=0, tiled=True)  13.7 us
    ppermute x7, starting transfers between devices, on_device(): screens.append(lax.ppermute(screen_sends[distance], near_axes, to))  9.47 us
  transfers between devices with their start and end apart: 8, of which 0 were waited for; matrix products, arithmetic and copies ran while one was open for 0% of the time, Pallas kernels for 15%

commit v1 on v0

--- a/solution.py
+++ b/solution.py
@@ -55,7 +55,8 @@
     )(*arrays)
 
 
-def pack_kernel(kpts_ref, orbital_ref, trial_ref, out_ref, room, fetch_sems, send_sems):
+def pack_kernel(kpts_ref, q_ref, orbital_ref, trial_ref, screen_ref, out_ref, *refs):
+    *sends, room, table, ordered, fetch_sems, send_sems, table_sem = refs
     bx, bc = lax.axis_index("bx"), lax.axis_index("bc")
     strips, low = lax.axis_size("bx"), room.shape[0]
     points = orbital_ref.shape[2]
@@ -72,18 +73,38 @@
         fetches.append([pltpu.make_async_copy(x, y, fetch_sems.at[d, k]) for k, (x, y) in enumerate(parts)])
         for fetch in fetches[-1]:
             fetch.start()
-    sends = []
+    table_fetch = pltpu.make_async_copy(screen_ref, table, table_sem)
+    table_fetch.start()
+    copies = []
     for d in range(low):
         for fetch in fetches[d]:
             fetch.wait()
         for h in range(out_ref.shape[0] // low):
-            sends.append(pltpu.make_async_copy(room.at[d], out_ref.at[h * low + d], send_sems.at[h, d]))
-            sends[-1].start()
-    for send in sends:
-        send.wait()
-
-
-def basis_kernel(out_ref, cos_low, sin_low, cos_high, sin_high, rows, sems):
+            copies.append(pltpu.make_async_copy(room.at[d], out_ref.at[h * low + d], send_sems.at[h, d]))
+            copies[-1].start()
+    table_fetch.wait()
+    me = lax.axis_index(("pl", "bx"))
+    rows, columns = sends[0].shape
+    kinds = screen_ref.shape[0] // rows
+    source = lax.broadcasted_iota(jnp.int32, (columns, columns), 0)
+    target = lax.broadcasted_iota(jnp.int32, (columns, columns), 1)
+    wanted = target % (columns // 2) * 2 + target // (columns // 2)
+    order = jnp.where(source == wanted, 1.0, 0.0).astype(BF16)
+    result = dot(table[...], order)
+    for t in range(columns // LANES):
+        ordered[t] = result[:, t * LANES : (t + 1) * LANES]
+    for distance, send in zip(distances(len(sends)), sends):
+        q = q_ref[me ^ own_distance(distance)]
+        for odd in range(2):
+            for t in range(columns // LANES):
+                send[odd * rows // 2 : (odd + 1) * rows // 2, t * LANES : (t + 1) * LANES] = ordered[
+                    t, pl.ds(q + kinds * odd, rows // 2, stride=2 * kinds), :
+                ].astype(BF16)
+    for copy in copies:
+        copy.wait()
+
+
+def basis_kernel(rows, cos_low, sin_low, cos_high, sin_high):
     columns = rows.shape[1]
     quarter = columns // 4
     groups = lax.axis_size("bc")
@@ -117,74 +138,40 @@
 
     table(2, 1, cos_low, sin_low, math.sqrt(2.0 / NR))
     table(2 * TABLE, 0, cos_high, sin_high, 1.0)
-    parts = sems.shape[0]
-    blocks = rows.shape[0] // TABLE // parts
-    copies = []
-    for part in range(parts):
-
-        def step(block, carry):
-            high = pl.ds(block, 1)
-            value = cos_low[...] * cos_high[high, :] - sin_low[...] * sin_high[high, :]
-            rows[pl.ds(pl.multiple_of(block * TABLE, TABLE), TABLE), :] = value.astype(BF16)
-            return carry
-
-        lax.fori_loop(part * blocks, (part + 1) * blocks, step, 0)
-        span = pl.ds(part * blocks * TABLE, blocks * TABLE)
-        copies.append(pltpu.make_async_copy(rows.at[span, :], out_ref.at[span, :], sems.at[part]))
-        copies[-1].start()
-    for copy in copies:
-        copy.wait()
-
-
-def select_kernel(q_ref, screen_ref, *refs):
-    sends, ordered = refs[:-1], refs[-1]
-    me = lax.axis_index(("pl", "bx"))
-    rows, columns = sends[0].shape
-    kinds = screen_ref.shape[0] // rows
-    source = lax.broadcasted_iota(jnp.int32, (columns, columns), 0)
-    target = lax.broadcasted_iota(jnp.int32, (columns, columns), 1)
-    wanted = target % (columns // 2) * 2 + target // (columns // 2)
-    order = jnp.where(source == wanted, 1.0, 0.0).astype(BF16)
-    result = dot(screen_ref[...], order)
-    for t in range(columns // LANES):
-        ordered[t] = result[:, t * LANES : (t + 1) * LANES]
-    for distance, send in enumerate(sends):
-        q = q_ref[me ^ distance]
-        for odd in range(2):
-            for t in range(columns // LANES):
-                send[odd * rows // 2 : (odd + 1) * rows // 2, t * LANES : (t + 1) * LANES] = ordered[
-                    t, pl.ds(q + kinds * odd, rows // 2, stride=2 * kinds), :
-                ].astype(BF16)
-
-
-def transform_kernel(
-    own_ref,
-    other_ref,
-    basis_ref,
-    val_ref,
-    cond_ref,
-    first,
-    second,
-    even,
-    odd,
-    basis,
-    conduction,
-    sems,
-):
+
+    def step(block, carry):
+        high = pl.ds(block, 1)
+        value = cos_low[...] * cos_high[high, :] - sin_low[...] * sin_high[high, :]
+        rows[pl.ds(pl.multiple_of(block * TABLE, TABLE), TABLE), :] = value.astype(BF16)
+        return carry
+
+    lax.fori_loop(0, rows.shape[0] // TABLE, step, 0)
+
+
+def distances(count):
+    order = [0] + [d for d in (1, 7, 5, 3, 6, 4, 2) if d < count]
+    order += [d for d in range(1, count) if d not in order]
+    return [(d, (d << 1) % count | (d << 1) // count) for d in order]
+
+
+def own_distance(pair):
+    return jnp.where(lax.axis_index("bc") % 2 == 0, pair[0], pair[1])
+
+
+def pair_kernel(own_ref, other_ref, basis_ref, *refs):
+    *screens, out_ref, first, second, even, odd, valence, conduction, screen, screened = refs[:-4]
+    slabs, vectors, diagonal, sides = refs[-4:]
     side = lax.axis_index("bc")
-    blocks, _, _ = own_ref.shape
+    blocks, count, width = own_ref.shape
     points = NR // blocks
+    states = NVC // blocks
     piece = 256 if points % 256 == 0 else LANES
     middle = NR // 2
-    half = val_ref.shape[1]
+    half = valence.shape[1]
     quarter = half // 2
     strips = lax.axis_size("bx")
     run = quarter // strips
-    fetches = [
-        pltpu.make_async_copy(basis_ref.at[:, pl.ds(k * half, half)], basis.at[k], sems.at[k]) for k in range(2)
-    ]
-    fetches[1].start()
-    fetches[0].start()
+    broad = screen.shape[2]
     source = lax.broadcasted_iota(jnp.int32, (piece, piece), 0)
     target = lax.broadcasted_iota(jnp.int32, (piece, piece), 1)
     flip = jnp.where(source + target == piece - 1, 1.0, 0.0).astype(BF16)
@@ -197,51 +184,16 @@
                 first[slot, half_of, :, start : start + piece] = value[:NV]
                 second[slot, half_of, :, start : start + piece] = value[NV:]
 
-    store = pltpu.make_async_copy(conduction, cond_ref, sems.at[2])
-    for kind in (1, 0):
-        outer, inner = (second, first) if kind else (first, second)
-        for v in range(NV):
-            rows = slice(v * NV, (v + 1) * NV)
-            ahead = outer[kind, 0, v : v + 1, :] * inner[kind, 0]
-            behind = outer[kind, 1, v : v + 1, :] * inner[kind, 1]
-            even[kind, rows, :] = (ahead + behind).astype(BF16)
-            odd[kind, rows, :] = (ahead - behind).astype(BF16)
-        fetches[kind].wait()
-        for parity, density in enumerate((even, odd)):
-            result = dot(density[kind], basis[kind, :, parity * quarter : (parity + 1) * quarter]).astype(BF16)
-            if kind == 0:
-                val_ref[:, parity * quarter : (parity + 1) * quarter] = result
-            else:
-                for s in range(strips):
-                    to = (2 * s + parity) * run
-                    conduction[:, to : to + run] = result[:, s * run : (s + 1) * run]
-        if kind == 1:
-            store.start()
-    store.wait()
-
-
-def apply_kernel(own_ref, other_ref, val_ref, cond_ref, *refs):
-    *screens, out_ref, screen, screened, slabs, vectors, diagonal, conduction, sides, sem = refs
-    fetch = pltpu.make_async_copy(cond_ref, conduction, sem)
-    fetch.start()
-    side = lax.axis_index("bc")
-    blocks, count, width = own_ref.shape
-    states = NVC // blocks
-    half = val_ref.shape[1]
-    strips = lax.axis_size("bx")
-    broad = screen.shape[2]
     if len(screens) > 1:
         me = lax.axis_index(("pl", "bx"))
         part = screens[0].shape[0] // 2
-        for distance, ref in enumerate(screens):
-            origin = me ^ distance
-            for odd in range(2):
-                at = pl.multiple_of(odd * (half // 2) + origin // strips * part, part)
-                screen[origin % strips, pl.ds(at, part), :] = ref[odd * part : (odd + 1) * part, :]
+        for distance, ref in zip(distances(len(screens)), screens):
+            origin = me ^ own_distance(distance)
+            for parity in range(2):
+                at = pl.multiple_of(parity * quarter + origin // strips * part, part)
+                screen[origin % strips, pl.ds(at, part), :] = ref[parity * part : (parity + 1) * part, :]
     else:
         screen[...] = screens[0][...]
-    for s in range(strips):
-        screened[:, s * broad : (s + 1) * broad] = dot(val_ref[...], screen[s]).astype(BF16)
 
     repeat = LANES // NV
     lanes = repeat * count
@@ -252,6 +204,33 @@
         for slot, ref in ((side, own_ref), (1 - side, other_ref)):
             turned = ref[b, :, width - states :].astype(F32).T
             vectors[slot, b * states : (b + 1) * states, :] = jnp.concatenate([turned] * fold, axis=1)
+    for kind in range(2):
+        for j in range(NC):
+            rows = vectors[1, pl.ds(j, NV, stride=NV), :] if kind == 0 else vectors[0, j * NC : (j + 1) * NC, :]
+            rows = jnp.concatenate([rows.astype(BF16)] * (lanes // LANES), axis=1)
+            for r in range(repeat):
+                diagonal[kind, j * LANES + r * NV : j * LANES + (r + 1) * NV, :] = rows * masks[r]
+
+    for kind in (1, 0):
+        outer, inner = (second, first) if kind else (first, second)
+        for v in range(NV):
+            rows = slice(v * NV, (v + 1) * NV)
+            ahead = outer[kind, 0, v : v + 1, :] * inner[kind, 0]
+            behind = outer[kind, 1, v : v + 1, :] * inner[kind, 1]
+            even[kind, rows, :] = (ahead + behind).astype(BF16)
+            odd[kind, rows, :] = (ahead - behind).astype(BF16)
+        for parity, density in enumerate((even, odd)):
+            at = (2 * kind + parity) * quarter
+            result = dot(density[kind], basis_ref[:, at : at + quarter]).astype(BF16)
+            if kind == 0:
+                valence[:, parity * quarter : (parity + 1) * quarter] = result
+            else:
+                for s in range(strips):
+                    to = (2 * s + parity) * run
+                    conduction[:, to : to + run] = result[:, s * run : (s + 1) * run]
+    for s in range(strips):
+        screened[:, s * broad : (s + 1) * broad] = dot(valence[...], screen[s]).astype(BF16)
+
     groups = NVC // LANES
     scale = 1.0 / math.sqrt(NVC) / math.sqrt(NG)
     source = lax.broadcasted_iota(jnp.int32, (LANES, LANES), 0)
@@ -267,13 +246,7 @@
             for b in range(out_ref.shape[1]):
                 out_ref[to, b, kind, :, at : at + LANES] = value[b * share : (b + 1) * share]
 
-    fetch.wait()
     for kind in range(2):
-        for j in range(NC):
-            rows = vectors[1, pl.ds(j, NV, stride=NV), :] if kind == 0 else vectors[0, j * NC : (j + 1) * NC, :]
-            rows = jnp.concatenate([rows.astype(BF16)] * (lanes // LANES), axis=1)
-            for r in range(repeat):
-                diagonal[kind, j * LANES + r * NV : j * LANES + (r + 1) * NV, :] = rows * masks[r]
         left, right = (conduction, screened) if kind == 0 else (screened, conduction)
         raw = dot_rows(left[...], right[...]).astype(BF16)
         for j in range(NC):
@@ -329,26 +302,29 @@
     states, _, count = trial.shape
     tall, kinds, broad = screening.shape
     half = NG // HALVES
-    aligned = points % LANES == 0 and states % LANES == 0
+    aligned = points % LANES == 0 and states % LANES == 0 and pair_count & (pair_count - 1) == 0
     orbital_t, trial_t = orbitals.transpose(1, 2, 0), trial.transpose(1, 2, 0)
     kpts_t = pair_kpts.T
 
     if aligned:
-        send = call(
+        send, *screen_sends = call(
             pack_kernel,
-            [("s", kpts_t), ("h", orbital_t), ("h", trial_t)],
-            [("h", (pair_count, count, points + states), BF16)],
+            [
+                ("s", kpts_t),
+                ("s", pair_q),
+                ("h", orbital_t),
+                ("h", trial_t),
+                ("h", screening.reshape(tall * kinds, broad)),
+            ],
+            [("h", (pair_count, count, points + states), BF16)] + [("b", (tall, broad), BF16)] * (low * strips),
             [
                 pltpu.VMEM((low, count, points + states), BF16),
+                pltpu.VMEM((tall * kinds, broad), BF16),
+                pltpu.VMEM((broad // LANES, tall * kinds, LANES), F32),
                 pltpu.SemaphoreType.DMA((low, 3)),
                 pltpu.SemaphoreType.DMA((halves, low)),
+                pltpu.SemaphoreType.DMA,
             ],
-        )[0]
-        screen_sends = call(
-            select_kernel,
-            [("s", pair_q), ("b", screening.reshape(tall * kinds, broad))],
-            [("b", (tall, broad), BF16)] * (low * strips),
-            [pltpu.VMEM((broad // LANES, tall * kinds, LANES), F32)],
             flops=NG * NG * 256,
         )
     else:
@@ -364,17 +340,17 @@
     basis = call(
         basis_kernel,
         [],
-        [("h", (NR // 2, 2 * half), BF16)],
-        [pltpu.VMEM((TABLE, 2 * half), F32)] * 4
-        + [pltpu.VMEM((NR // 2, 2 * half), BF16), pltpu.SemaphoreType.DMA((4,))],
+        [("v", (NR // 2, 2 * half), BF16)],
+        [pltpu.VMEM((TABLE, 2 * half), F32)] * 4,
         flops=NR * NG * 8,
     )[0]
     if aligned:
-        near_axes = ("pl", "bx")
         screens = list(screen_sends[:1])
-        for distance in range(1, low * strips):
-            to = [(i, i ^ distance) for i in range(low * strips)]
-            screens.append(lax.ppermute(screen_sends[distance], near_axes, to))
+        for step, distance in list(enumerate(distances(low * strips)))[1:]:
+            to = [
+                (i * groups + g, (i ^ distance[g % 2]) * groups + g) for i in range(low * strips) for g in range(groups)
+            ]
+            screens.append(lax.ppermute(screen_sends[step], ("pl", "bx", "bc"), to))
     else:
         screen_got = lax.all_to_all(screen_send, ("pl", "bx"), split_axis=0, concat_axis=0, tiled=True)
     other = lax.ppermute(got, "bc", [(i, i ^ 1) for i in range(groups)])
@@ -391,38 +367,27 @@
         screen_got = screen_got.reshape(low, strips, tall // 2, 2, broad // 2, 2).transpose(1, 3, 0, 2, 5, 4)
         screens = [screen_got.reshape(strips, low * tall, broad)]
 
-    valence, conduction = call(
-        transform_kernel,
-        [("v", got), ("v", other), ("h", basis)],
-        [("v", (NVC, half), BF16), ("h", (NVC, half), BF16)],
+    share = count // (strips * groups)
+    lanes = LANES // NV * count
+    partial = call(
+        pair_kernel,
+        [("v", got), ("v", other), ("v", basis)] + [("v", x) for x in screens],
+        [("v", (pair_count, strips * groups, 2, share, states) if aligned else (2, count, NVC), BF16)],
         [
             pltpu.VMEM((2, 2, NV, NR // 2), F32),
             pltpu.VMEM((2, 2, NV, NR // 2), F32),
             pltpu.VMEM((2, NVC, NR // 2), BF16),
             pltpu.VMEM((2, NVC, NR // 2), BF16),
-            pltpu.VMEM((2, NR // 2, half), BF16),
             pltpu.VMEM((NVC, half), BF16),
-            pltpu.SemaphoreType.DMA((3,)),
-        ],
-        flops=2 * NVC * NR * half,
-    )
-    share = count // (strips * groups)
-    lanes = LANES // NV * count
-    partial = call(
-        apply_kernel,
-        [("v", got), ("v", other), ("v", valence), ("h", conduction)] + [("v", x) for x in screens],
-        [("v", (pair_count, strips * groups, 2, share, states) if aligned else (2, count, NVC), BF16)],
-        [
+            pltpu.VMEM((NVC, half), BF16),
             pltpu.VMEM((strips, half, broad), BF16),
             pltpu.VMEM((NVC, half), BF16),
             pltpu.VMEM((2, NVC // LANES * NC, NC * LANES), BF16),
             pltpu.VMEM((2, NVC, LANES), F32),
             pltpu.VMEM((2, NC * LANES, lanes), BF16),
-            pltpu.VMEM((NVC, half), BF16),
             pltpu.VMEM((lanes // LANES, NVC // LANES * NC, LANES), F32),
-            pltpu.SemaphoreType.DMA,
         ],
-        flops=2 * NVC * half * half + 8 * NVC * NVC * half,
+        flops=2 * NVC * NR * half + 2 * NVC * half * half + 8 * NVC * NVC * half,
     )[0]
     if not aligned:
         partial = partial.reshape(2, strips * groups, share, pair_count, states).transpose(3, 1, 0, 2, 4)

time: 63.2 us -> 58.3 us (0.922)
  Pallas kernels: 20.1 us -> 13.8 us
  waiting for transfers between devices: 0.02 us -> 3.28 us
  starting transfers between devices: 9.47 us -> 8.15 us
    pallas_call x6 -> x4, Pallas kernels: 20.1 us -> 13.8 us  [call(): pl.pallas_call(body, out_shape=shapes, in_specs=specs, out_specs=out_spec...]
    ppermute x7, waiting for transfers between devices: 0.02 us -> 3.27 us  [on_device(): screens.append(lax.ppermute(screen_sends[step], ('pl', 'bx', 'bc'), to))]
    ppermute x7, starting transfers between devices: 9.47 us -> 8.15 us  [on_device(): screens.append(lax.ppermute(screen_sends[step], ('pl', 'bx', 'bc'), to))]
  transfers between devices with their start and end apart: 8 -> 8, of which waited for: 0 -> 4; matrix products, arithmetic and copies ran while one was open for 0% -> 0% of each run, Pallas kernels for 15% -> 2%
where the time goes in v1:
time: 58.3 us; the launch traced here: 58 us
  blocking collectives  32.8 us (56%)
  Pallas kernels  13.8 us (24%)
  starting transfers between devices  8.15 us (14%)
  waiting for transfers between devices  3.28 us (6%)
    all_to_all x1, blocking collectives, on_device(): lax.all_to_all(send, pair_axes, split_axis=0, concat_axis=0, tiled=True)  19.4 us
    pallas_call x4, Pallas kernels, call(): pl.pallas_call(body, out_shape=shapes, in_specs=specs, out_specs=out_spec...  13.8 us
    all_to_all x1, blocking collectives, on_device(): lax.all_to_all(out_send, all_axes, split_axis=0, concat_axis=0, tiled=True)  13.4 us
    ppermute x7, starting transfers between devices, on_device(): screens.append(lax.ppermute(screen_sends[step], ('pl', 'bx', 'bc'), to))  8.15 us
    ppermute x7, waiting for transfers between devices, on_device(): screens.append(lax.ppermute(screen_sends[step], ('pl', 'bx', 'bc'), to))  3.27 us
  transfers between devices with their start and end apart: 8, of which 4 were waited for; matrix products, arithmetic and copies ran while one was open for 0% of the time, Pallas kernels for 2%

profile of v1, /device:TPU:0, one launch (start us, length us, event | category | flops | bytes accessed | tf_op | source)
XLA Modules:
  0.0 58.0 jit_solution(17815121159081988308)
XLA Ops:
  0.0 2.8 %shard_map.55 = (bf16[8,64,384]{2,1,0:T(8,128)(2,1)}, bf16[128,256]{1,0:T(8,128)(2,1)S(1)}, bf16[128,256]{1,0:T(8,128)(2,1)S(1)}, bf16[128,256]{1,0:T(8,128)(2,1...) custom-call(s32[2,8]{1,0:T(2,128)} %bitcast.12, ...), custom_call_target="tpu_custom_call" | custom-call | flops 268435456 | bytes 1048576 | tf_op jit(solution)/shard_map/pallas_call | solution.py:47
  2.8 19.4 %all_to_all.10.own_ref = bf16[8,64,384]{2,1,0:T(8,128)(2,1)S(1)} all-to-all(bf16[8,64,384]{2,1,0:T(8,128)(2,1)} %get-tuple-element.14), channel_id=1, replica_groups=mesh['ph'=2,'pl'=4,'bx'=2,'bc'=2] {'ph','pl'}, dimensions={0} | all-to-all | bytes 786432 | tf_op jit(solution)/shard_map/all_to_all | solution.py:339
  22.2 0.0 collective-permute-start
  22.2 1.5 %collective-permute-start.1 = (bf16[128,256]{1,0:T(8,128)(2,1)S(1)}, bf16[128,256]{1,0:T(8,128)(2,1)S(1)}, u32[]{:S(2)}, u32[]{:S(2)}) collective-permute-start(bf16[128,256]{1,0:T(8,128)(2,1)S(1)} %get-tuple-element.16), channel_id=1, source_target_pairs={{0,2},{1,5},{2,0},{3,7},{4,6},{5,1},{6,4},{7,3},{8,10},{9,13},{10,... | collective-permute-start | bytes 196616 | tf_op jit(solution)/shard_map/ppermute | solution.py:353
  23.7 0.7 %collective-permute-start.2 = (bf16[128,256]{1,0:T(8,128)(2,1)S(1)}, bf16[128,256]{1,0:T(8,128)(2,1)S(1)}, u32[]{:S(2)}, u32[]{:S(2)}) collective-permute-start(bf16[128,256]{1,0:T(8,128)(2,1)S(1)} %get-tuple-element.17), channel_id=1, source_target_pairs={{0,14},{1,15},{2,12},{3,13},{4,10},{5,11},{6,8},{7,9},{8,6},{9,7},... | collective-permute-start | bytes 196616 | tf_op jit(solution)/shard_map/ppermute | solution.py:353
  24.4 2.7 %collective-permute-start.3 = (bf16[128,256]{1,0:T(8,128)(2,1)S(1)}, bf16[128,256]{1,0:T(8,128)(2,1)S(1)}, u32[]{:S(2)}, u32[]{:S(2)}) collective-permute-start(bf16[128,256]{1,0:T(8,128)(2,1)S(1)} %get-tuple-element.18), channel_id=1, source_target_pairs={{0,10},{1,7},{2,8},{3,5},{4,14},{5,3},{6,12},{7,1},{8,2},{9,15},{1... | collective-permute-start | bytes 196616 | tf_op jit(solution)/shard_map/ppermute | solution.py:353
  27.1 0.9 %collective-permute-start.4 = (bf16[128,256]{1,0:T(8,128)(2,1)S(1)}, bf16[128,256]{1,0:T(8,128)(2,1)S(1)}, u32[]{:S(2)}, u32[]{:S(2)}) collective-permute-start(bf16[128,256]{1,0:T(8,128)(2,1)S(1)} %get-tuple-element.19), channel_id=1, source_target_pairs={{0,6},{1,13},{2,4},{3,15},{4,2},{5,9},{6,0},{7,11},{8,14},{9,5},{1... | collective-permute-start | bytes 196616 | tf_op jit(solution)/shard_map/ppermute | solution.py:353
  28.0 0.0 collective-permute-done.1.refs_1_
  28.0 0.7 %collective-permute-start.5 = (bf16[128,256]{1,0:T(8,128)(2,1)S(1)}, bf16[128,256]{1,0:T(8,128)(2,1)S(1)}, u32[]{:S(2)}, u32[]{:S(2)}) collective-permute-start(bf16[128,256]{1,0:T(8,128)(2,1)S(1)} %get-tuple-element.20), channel_id=1, source_target_pairs={{0,12},{1,11},{2,14},{3,9},{4,8},{5,15},{6,10},{7,13},{8,4},{9,3},... | collective-permute-start | bytes 196616 | tf_op jit(solution)/shard_map/ppermute | solution.py:353
  28.8 1.5 %collective-permute-done.2.refs_2_ = bf16[128,256]{1,0:T(8,128)(2,1)S(1)} collective-permute-done((bf16[128,256]{1,0:T(8,128)(2,1)S(1)}, bf16[128,256]{1,0:T(8,128)(2,1)S(1)}, u32[]{:S(2)}, u32[]{:S(2)}) %collective-permute-start.2) | collective-permute-done | bytes 65568 | tf_op jit(solution)/shard_map/ppermute | solution.py:353
  30.3 0.4 collective-permute-start.6
  30.7 0.0 collective-permute-done.3.refs_3_
  30.7 1.1 %collective-permute-start.7 = (bf16[128,256]{1,0:T(8,128)(2,1)S(1)}, bf16[128,256]{1,0:T(8,128)(2,1)S(1)}, u32[]{:S(2)}, u32[]{:S(2)}) collective-permute-start(bf16[128,256]{1,0:T(8,128)(2,1)S(1)} %get-tuple-element.22), channel_id=1, source_target_pairs={{0,4},{1,9},{2,6},{3,11},{4,0},{5,13},{6,2},{7,15},{8,12},{9,1},{1... | collective-permute-start | bytes 196616 | tf_op jit(solution)/shard_map/ppermute | solution.py:353
  31.8 1.4 %shard_map.56.basis_ref = bf16[1024,1024]{1,0:T(8,128)(2,1)S(1)} custom-call(), custom_call_target="tpu_custom_call" | custom-call | flops 16777216 | bytes 1048576 | tf_op jit(solution)/shard_map/pallas_call | solution.py:47
  33.2 0.5 collective-permute-done.4.refs_4_
  33.7 0.0 collective-permute-done.5.refs_5_
  33.7 1.1 %collective-permute-done.6.refs_6_ = bf16[128,256]{1,0:T(8,128)(2,1)S(1)} collective-permute-done((bf16[128,256]{1,0:T(8,128)(2,1)S(1)}, bf16[128,256]{1,0:T(8,128)(2,1)S(1)}, u32[]{:S(2)}, u32[]{:S(2)}) %collective-permute-start.6) | collective-permute-done | bytes 65568 | tf_op jit(solution)/shard_map/ppermute | solution.py:353
  34.8 0.1 collective-permute-done.7.refs_7_
  35.0 0.0 collective-permute-done.other_ref
  35.0 8.2 %shard_map.57 = bf16[8,4,2,16,128]{4,3,2,1,0:T(8,128)(2,1)S(1)} custom-call(bf16[8,64,384]{2,1,0:T(8,128)(2,1)S(1)} %all_to_all.10.own_ref, bf16[8,64,384]{2,1,0:T(8,128)(2,1)S(1)} %collective-permute-done.other_ref, bf16[1024,1024]{1,0:T(8,128)(2,1)S(1)} %shard_map.56.basis_ref, bf16[128,256]{1,0:T(8,128)(2,1)S(1)} %get-tuple-element.15.refs_0_, ...), custom_call_target="tpu_custom_call" | custom-call | flops 6979321856 | bytes 1048576 | tf_op jit(solution)/shard_map/pallas_call | solution.py:47
  43.2 13.4 %all_to_all.11 = bf16[32,2,16,128]{3,2,1,0:T(8,128)(2,1)S(1)} all-to-all(bf16[32,2,16,128]{3,2,1,0:T(8,128)(2,1)S(1)} %bitcast.8), channel_id=1, replica_groups=mesh['ph'=2,'pl'=4,'bx'=2,'bc'=2] {'ph','pl','bx','bc'}, dimensions={0} | all-to-all | bytes 524288 | tf_op jit(solution)/shard_map/all_to_all | solution.py:395
  56.6 1.4 %shard_map.58 = f32[23,16,128]{2,1,0:T(8,128)} custom-call(s32[2,8]{1,0:T(2,128)} %bitcast.13, bf16[2,4,2,2,2,16,128]{6,5,4,3,2,1,0:T(8,128)(2,1)S(1)} %bitcast.7), custom_call_target="tpu_custom_call" | custom-call | bytes 1048576 | tf_op jit(solution)/shard_map/pallas_call | solution.py:47
Async XLA Ops:
  22.2 12.8 %collective-permute-start = (bf16[8,64,384]{2,1,0:T(8,128)(2,1)S(1)}, bf16[8,64,384]{2,1,0:T(8,128)(2,1)S(1)}, u32[]{:S(2)}, u32[]{:S(2)}) collective-permute-start(bf16[8,64,384]{2,1,0:T(8,128)(2,1)S(1)} %all_to_all.10.own_ref), channel_id=1, source_target_pairs={{0,1},{1,0},{2,3},{3,2},{4,5},{5,4},{6,7},{7,6},{8,9},{9,8},{10,11... | collective-permute-start | bytes 1179656 | tf_op jit(solution)/shard_map/ppermute | solution.py:356
  22.2 5.9 %collective-permute-start.1 = (bf16[128,256]{1,0:T(8,128)(2,1)S(1)}, bf16[128,256]{1,0:T(8,128)(2,1)S(1)}, u32[]{:S(2)}, u32[]{:S(2)}) collective-permute-start(bf16[128,256]{1,0:T(8,128)(2,1)S(1)} %get-tuple-element.16), channel_id=1, source_target_pairs={{0,2},{1,5},{2,0},{3,7},{4,6},{5,1},{6,4},{7,3},{8,10},{9,13},{10,... | collective-permute-start | bytes 196616 | tf_op jit(solution)/shard_map/ppermute | solution.py:353
  23.7 6.6 %collective-permute-start.2 = (bf16[128,256]{1,0:T(8,128)(2,1)S(1)}, bf16[128,256]{1,0:T(8,128)(2,1)S(1)}, u32[]{:S(2)}, u32[]{:S(2)}) collective-permute-start(bf16[128,256]{1,0:T(8,128)(2,1)S(1)} %get-tuple-element.17), channel_id=1, source_target_pairs={{0,14},{1,15},{2,12},{3,13},{4,10},{5,11},{6,8},{7,9},{8,6},{9,7},... | collective-permute-start | bytes 196616 | tf_op jit(solution)/shard_map/ppermute | solution.py:353
  24.4 6.3 %collective-permute-start.3 = (bf16[128,256]{1,0:T(8,128)(2,1)S(1)}, bf16[128,256]{1,0:T(8,128)(2,1)S(1)}, u32[]{:S(2)}, u32[]{:S(2)}) collective-permute-start(bf16[128,256]{1,0:T(8,128)(2,1)S(1)} %get-tuple-element.18), channel_id=1, source_target_pairs={{0,10},{1,7},{2,8},{3,5},{4,14},{5,3},{6,12},{7,1},{8,2},{9,15},{1... | collective-permute-start | bytes 196616 | tf_op jit(solution)/shard_map/ppermute | solution.py:353
  27.1 6.6 %collective-permute-start.4 = (bf16[128,256]{1,0:T(8,128)(2,1)S(1)}, bf16[128,256]{1,0:T(8,128)(2,1)S(1)}, u32[]{:S(2)}, u32[]{:S(2)}) collective-permute-start(bf16[128,256]{1,0:T(8,128)(2,1)S(1)} %get-tuple-element.19), channel_id=1, source_target_pairs={{0,6},{1,13},{2,4},{3,15},{4,2},{5,9},{6,0},{7,11},{8,14},{9,5},{1... | collective-permute-start | bytes 196616 | tf_op jit(solution)/shard_map/ppermute | solution.py:353
  28.0 5.7 %collective-permute-start.5 = (bf16[128,256]{1,0:T(8,128)(2,1)S(1)}, bf16[128,256]{1,0:T(8,128)(2,1)S(1)}, u32[]{:S(2)}, u32[]{:S(2)}) collective-permute-start(bf16[128,256]{1,0:T(8,128)(2,1)S(1)} %get-tuple-element.20), channel_id=1, source_target_pairs={{0,12},{1,11},{2,14},{3,9},{4,8},{5,15},{6,10},{7,13},{8,4},{9,3},... | collective-permute-start | bytes 196616 | tf_op jit(solution)/shard_map/ppermute | solution.py:353
  30.3 4.6 %collective-permute-start.6 = (bf16[128,256]{1,0:T(8,128)(2,1)S(1)}, bf16[128,256]{1,0:T(8,128)(2,1)S(1)}, u32[]{:S(2)}, u32[]{:S(2)}) collective-permute-start(bf16[128,256]{1,0:T(8,128)(2,1)S(1)} %get-tuple-element.21), channel_id=1, source_target_pairs={{0,8},{1,3},{2,10},{3,1},{4,12},{5,7},{6,14},{7,5},{8,0},{9,11},{1... | collective-permute-start | bytes 196616 | tf_op jit(solution)/shard_map/ppermute | solution.py:353
  30.7 4.3 %collective-permute-start.7 = (bf16[128,256]{1,0:T(8,128)(2,1)S(1)}, bf16[128,256]{1,0:T(8,128)(2,1)S(1)}, u32[]{:S(2)}, u32[]{:S(2)}) collective-permute-start(bf16[128,256]{1,0:T(8,128)(2,1)S(1)} %get-tuple-element.22), channel_id=1, source_target_pairs={{0,4},{1,9},{2,6},{3,11},{4,0},{5,13},{6,2},{7,15},{8,12},{9,1},{1... | collective-permute-start | bytes 196616 | tf_op jit(solution)/shard_map/ppermute | solution.py:353
